TPU v7x, 256 devices: a whole 4x4x8 slice. The times are simulated.
256 devices in a mesh: chan: 8 (over x, core), ctx: 32 (over z, y).
Axes of the slice: x: 4, y: 4, z: 8, core: 2. Of those that a mesh axis runs over, the one named last changes fastest.
Arguments:
- queries: bfloat16 [4096, 8192], P('ctx', 'chan'), may hold values from -6 to 6
- keys: bfloat16 [4096, 8192], P('ctx', 'chan'), may hold values from -6 to 6
- values: bfloat16 [4096, 8192], P('ctx', 'chan'), may hold values from -6 to 6
- filters: bfloat16 [4, 4096], P(None, 'ctx'), may hold values from -0.09375 to 0.09375
- cotangent: bfloat16 [4096, 8192], P('ctx', 'chan'), may hold values from -6 to 6
Outputs:
- output: bfloat16 [4096, 8192], P('ctx', 'chan')
- query_grad: bfloat16 [4096, 8192], P('ctx', 'chan')
- key_grad: bfloat16 [4096, 8192], P('ctx', 'chan')
- value_grad: bfloat16 [4096, 8192], P('ctx', 'chan')
- filter_grad: float32 [4, 4096], P(None, 'ctx')
All inputs are finite; a program needn't handle non-finite values.
Results may differ from a plain program's by a relative error of at most 0.015.
Values may be sent and summed in bfloat16 or wider, within the bound.
A program may use at most 64 MiB of HBM per device.

v0:
```python
import jax
import jax.numpy as jnp
from jax import lax
from jax.sharding import PartitionSpec as P

D = 8192
NFILT = 4


def toeplitz(padded, base, height, breadth):
    middle = padded.shape[1] // 2
    span = height + breadth - 1
    window = lax.dynamic_slice_in_dim(padded, middle + base - breadth + 1, span, 1)
    flipped = window[:, ::-1]
    tiled = jnp.tile(flipped, (1, height + 1))
    flat = tiled[:, height - 1 : height - 1 + height * (span - 1)]
    return flat.reshape(padded.shape[0], height, span - 1)[:, :, :breadth]


def diagonal_sums(product):
    nfil, height, breadth = product.shape
    stride = height + breadth
    flipped = product[:, :, ::-1]
    padded = jnp.pad(flipped, ((0, 0), (0, 0), (0, height)))
    flat = padded.reshape(nfil, height * stride)[:, : height * (stride - 1)]
    return jnp.sum(flat.reshape(nfil, height, stride - 1), axis=1)


def add_lags(lag_acc, sums, first_lag):
    middle = lag_acc.shape[1] // 2
    where = middle + first_lag
    current = lax.dynamic_slice_in_dim(lag_acc, where, sums.shape[1], 1)
    return lax.dynamic_update_slice_in_dim(lag_acc, current + sums, where, 1)


def in_blocks(block_fn, carry, piece, rows):
    count = piece.shape[0]
    size = rows * max(1, 512 // rows)
    parts = piece.reshape((count // size, size) + piece.shape[1:])
    offsets = jnp.arange(count // size, dtype=jnp.int32) * size

    def visit(state, item):
        block, offset = item
        return (block_fn(state, block, offset), None)

    result, unused = lax.scan(visit, carry, (parts, offsets))
    return result


def shards(queries, keys, values, filters, cotangent):
    rows, width = queries.shape
    nfil = filters.shape[0]
    narrow = width // nfil
    gated = (keys.astype(jnp.float32) * values.astype(jnp.float32)).astype(jnp.bfloat16)
    back = (cotangent.astype(jnp.float32) * queries.astype(jnp.float32)).astype(jnp.bfloat16)
    taps = lax.all_gather(filters, "ctx", axis=1, tiled=True)
    total = taps.shape[1]
    padded = jnp.concatenate([jnp.zeros_like(taps), taps], axis=1)
    lag_start = jnp.zeros((nfil, 2 * total), jnp.float32)
    first = lax.axis_index("ctx") * rows
    back_cols = back.reshape(rows, narrow, nfil)

    def forward_block(carry, piece, start):
        count = piece.shape[0]

        def forward_work(state):
            mixed_acc, lag_acc = state
            tile = toeplitz(padded, first - start, rows, count)
            columns = piece.reshape(count, narrow, nfil)
            mixed_acc = mixed_acc + jnp.einsum(
                "fst,tcf->scf", tile, columns, preferred_element_type=jnp.float32
            )
            product = jnp.einsum(
                "scf,tcf->fst", back_cols, columns, preferred_element_type=jnp.float32
            )
            lag_acc = add_lags(lag_acc, diagonal_sums(product), first - start - count + 1)
            return (mixed_acc, lag_acc)

        return lax.cond(start < first + rows, forward_work, lambda state: state, carry)

    empty = jnp.zeros((rows, narrow, nfil), jnp.float32)
    mixed_acc, lag_part = in_blocks(
        forward_block, (empty, lag_start), lax.all_gather(gated, "ctx", axis=0, tiled=True), rows
    )

    def backward_block(grad_acc, piece, start):
        count = piece.shape[0]

        def backward_work(state):
            tile = toeplitz(padded, start - first, count, rows)
            columns = piece.reshape(count, narrow, nfil)
            return state + jnp.einsum(
                "fst,scf->tcf", tile, columns, preferred_element_type=jnp.float32
            )

        return lax.cond(start + count > first, backward_work, lambda state: state, grad_acc)

    grad_acc = in_blocks(
        backward_block, empty, lax.all_gather(back, "ctx", axis=0, tiled=True), rows
    )
    mixed = mixed_acc.reshape(rows, width)
    gated_grad = grad_acc.reshape(rows, width)
    lag_share = lax.psum_scatter(
        lag_part[:, total:].astype(jnp.bfloat16), "ctx", scatter_dimension=1, tiled=True
    ).astype(jnp.float32)
    lag_total = lax.psum(lag_share, "chan")
    scale = (total * (D // NFILT)) ** (-0.5)
    filter_grad = lag_total * scale
    output = (queries.astype(jnp.float32) * mixed).astype(jnp.bfloat16)
    query_grad = (cotangent.astype(jnp.float32) * mixed).astype(jnp.bfloat16)
    key_grad = (gated_grad * values.astype(jnp.float32)).astype(jnp.bfloat16)
    value_grad = (gated_grad * keys.astype(jnp.float32)).astype(jnp.bfloat16)
    return (output, query_grad, key_grad, value_grad, filter_grad)


def solution(mesh):
    placed = (
        P("ctx", "chan"),
        P("ctx", "chan"),
        P("ctx", "chan"),
        P(None, "ctx"),
        P("ctx", "chan"),
    )
    return jax.shard_map(
        shards,
        mesh=mesh,
        in_specs=placed,
        out_specs=(
            P("ctx", "chan"),
            P("ctx", "chan"),
            P("ctx", "chan"),
            P("ctx", "chan"),
            P(None, "ctx"),
        ),
        check_vma=False,
    )
```

profile of v0, /device:TPU:1, one launch (start us, length us, event | category | flops | bytes accessed | tf_op | source)
XLA Modules:
  0.0 846.8 jit_solution(6806432111096197766)
XLA Ops:
  12.5 38.3 %all_gather.9 = bf16[4,4096]{1,0:T(4,128)(2,1)S(1)} all-gather(bf16[4,128]{1,0:T(4,128)(2,1)S(1)} %copy-done.7), channel_id=1, replica_groups=mesh['chan'=8,'ctx'=32] {'ctx'}, dimensions={1}, use_global_device_ids=true | all-gather | bytes 33792 | tf_op jit(solution)/shard_map/all_gather | solution.py:56
  50.8 65.4 %all-gather.5.cloned.1.call-done = bf16[4096,1024]{0,1:T(8,128)(2,1)} async-done(((bf16[128,1024]{0,1:T(8,128)(2,1)}), bf16[4096,1024]{0,1:T(8,128)(2,1)}) %all-gather.5.cloned.1.call-update) | async-done | bytes 8388624 | tf_op jit(solution)/shard_map/all_gather | solution.py:99
  116.2 7.4 copy.60
  123.7 238.9 %while.27 = (s32[]{:T(128)}, f32[128,256,4]{1,0,2:T(8,128)S(1)}, s32[8]{0:T(128)S(1)}, s32[]{:T(128)}, bf16[4,8192]{1,0:T(4,128)(2,1)S(1)}, /*index=5*/bf16[8,512,1024]{1,2,0:T(8,128)(2,1)}, s32[]{:T(128)}, s32[]{:T(128)}) while((s32[]{:T(128)}, f32[128,256,4]{1,0,2:T(8,128)S(1)}, s32[8]{0:T(128)S(1)}, s32[]{:T(128)}, ...), condition=%wide.region_8.9_spmd, body=%wide.region_5.8_spmd.sunk | while | flops 134348800 | bytes 35643552 | solution.py:46
  125.0 28.5 %conditional.5 = (f32[128,256,4]{1,0,2:T(8,128)S(1)}) conditional(s32[]{:T(128)} %convert_element_type.91, f32[128,256,4]{1,0,2:T(8,128)S(1)} %get-tuple-element.399, (s32[]{:T(128)}, s32[]{:T(128)}, bf16[4,8192]{1,0:T(4,128)(2,1)S(1)}, bf16[8,512,1024]{1,2,0:T(8,128)(2,1)}, s32[]{:T(128)}, /*index=5*/f32[128,256,4]{1,0,2:T(8,128)S(1)}) %tuple.73), branch_computations={%region_6.6_spmd, %region_7.7_spmd} | conditional | flops 134348800 | bytes 35643384 | solution.py:96
  126.6 6.1 reshape.68
  143.5 6.8 reshape.54
  154.9 28.5 %conditional.5 = (f32[128,256,4]{1,0,2:T(8,128)S(1)}) conditional(s32[]{:T(128)} %convert_element_type.91, f32[128,256,4]{1,0,2:T(8,128)S(1)} %get-tuple-element.399, (s32[]{:T(128)}, s32[]{:T(128)}, bf16[4,8192]{1,0:T(4,128)(2,1)S(1)}, bf16[8,512,1024]{1,2,0:T(8,128)(2,1)}, s32[]{:T(128)}, /*index=5*/f32[128,256,4]{1,0,2:T(8,128)S(1)}) %tuple.73), branch_computations={%region_6.6_spmd, %region_7.7_spmd} | conditional | flops 134348800 | bytes 35643384 | solution.py:96
  156.5 6.1 reshape.68
  173.4 6.8 reshape.54
  184.8 28.5 %conditional.5 = (f32[128,256,4]{1,0,2:T(8,128)S(1)}) conditional(s32[]{:T(128)} %convert_element_type.91, f32[128,256,4]{1,0,2:T(8,128)S(1)} %get-tuple-element.399, (s32[]{:T(128)}, s32[]{:T(128)}, bf16[4,8192]{1,0:T(4,128)(2,1)S(1)}, bf16[8,512,1024]{1,2,0:T(8,128)(2,1)}, s32[]{:T(128)}, /*index=5*/f32[128,256,4]{1,0,2:T(8,128)S(1)}) %tuple.73), branch_computations={%region_6.6_spmd, %region_7.7_spmd} | conditional | flops 134348800 | bytes 35643384 | solution.py:96
  186.3 6.1 reshape.68
  203.2 6.8 reshape.54
  214.6 28.5 %conditional.5 = (f32[128,256,4]{1,0,2:T(8,128)S(1)}) conditional(s32[]{:T(128)} %convert_element_type.91, f32[128,256,4]{1,0,2:T(8,128)S(1)} %get-tuple-element.399, (s32[]{:T(128)}, s32[]{:T(128)}, bf16[4,8192]{1,0:T(4,128)(2,1)S(1)}, bf16[8,512,1024]{1,2,0:T(8,128)(2,1)}, s32[]{:T(128)}, /*index=5*/f32[128,256,4]{1,0,2:T(8,128)S(1)}) %tuple.73), branch_computations={%region_6.6_spmd, %region_7.7_spmd} | conditional | flops 134348800 | bytes 35643384 | solution.py:96
  216.2 6.1 reshape.68
  233.1 6.8 reshape.54
  244.5 28.5 %conditional.5 = (f32[128,256,4]{1,0,2:T(8,128)S(1)}) conditional(s32[]{:T(128)} %convert_element_type.91, f32[128,256,4]{1,0,2:T(8,128)S(1)} %get-tuple-element.399, (s32[]{:T(128)}, s32[]{:T(128)}, bf16[4,8192]{1,0:T(4,128)(2,1)S(1)}, bf16[8,512,1024]{1,2,0:T(8,128)(2,1)}, s32[]{:T(128)}, /*index=5*/f32[128,256,4]{1,0,2:T(8,128)S(1)}) %tuple.73), branch_computations={%region_6.6_spmd, %region_7.7_spmd} | conditional | flops 134348800 | bytes 35643384 | solution.py:96
  246.1 6.1 reshape.68
  263.0 6.8 reshape.54
  274.4 28.5 %conditional.5 = (f32[128,256,4]{1,0,2:T(8,128)S(1)}) conditional(s32[]{:T(128)} %convert_element_type.91, f32[128,256,4]{1,0,2:T(8,128)S(1)} %get-tuple-element.399, (s32[]{:T(128)}, s32[]{:T(128)}, bf16[4,8192]{1,0:T(4,128)(2,1)S(1)}, bf16[8,512,1024]{1,2,0:T(8,128)(2,1)}, s32[]{:T(128)}, /*index=5*/f32[128,256,4]{1,0,2:T(8,128)S(1)}) %tuple.73), branch_computations={%region_6.6_spmd, %region_7.7_spmd} | conditional | flops 134348800 | bytes 35643384 | solution.py:96
  292.8 6.8 reshape.54
  304.2 28.5 %conditional.5 = (f32[128,256,4]{1,0,2:T(8,128)S(1)}) conditional(s32[]{:T(128)} %convert_element_type.91, f32[128,256,4]{1,0,2:T(8,128)S(1)} %get-tuple-element.399, (s32[]{:T(128)}, s32[]{:T(128)}, bf16[4,8192]{1,0:T(4,128)(2,1)S(1)}, bf16[8,512,1024]{1,2,0:T(8,128)(2,1)}, s32[]{:T(128)}, /*index=5*/f32[128,256,4]{1,0,2:T(8,128)S(1)}) %tuple.73), branch_computations={%region_6.6_spmd, %region_7.7_spmd} | conditional | flops 134348800 | bytes 35643384 | solution.py:96
  322.7 6.8 reshape.54
  334.1 28.5 %conditional.5 = (f32[128,256,4]{1,0,2:T(8,128)S(1)}) conditional(s32[]{:T(128)} %convert_element_type.91, f32[128,256,4]{1,0,2:T(8,128)S(1)} %get-tuple-element.399, (s32[]{:T(128)}, s32[]{:T(128)}, bf16[4,8192]{1,0:T(4,128)(2,1)S(1)}, bf16[8,512,1024]{1,2,0:T(8,128)(2,1)}, s32[]{:T(128)}, /*index=5*/f32[128,256,4]{1,0,2:T(8,128)S(1)}) %tuple.73), branch_computations={%region_6.6_spmd, %region_7.7_spmd} | conditional | flops 134348800 | bytes 35643384 | solution.py:96
  335.6 6.1 reshape.68
  352.6 6.8 reshape.54
  366.8 96.9 %all-gather.3.cloned.1.call-done = bf16[4096,1024]{0,1:T(8,128)(2,1)} async-done(((bf16[128,1024]{0,1:T(8,128)(2,1)}), bf16[4096,1024]{0,1:T(8,128)(2,1)}) %all-gather.3.cloned.1.call-update) | async-done | bytes 8388624 | tf_op jit(solution)/shard_map/all_gather | solution.py:83
  463.7 7.4 copy.61
  471.9 26.2 %while.26 = (s32[]{:T(128)}, f32[128,256,4]{1,0,2:T(8,128)}, f32[4,8192]{1,0:T(4,128)S(1)}, s32[8]{0:T(128)S(1)}, s32[]{:T(128)}, /*index=5*/s32[]{:T(128)}, bf1...) while((s32[]{:T(128)}, f32[128,256,4]{1,0,2:T(8,128)}, ...), condition=%wide.region_4.5_spmd, body=%wide.region_0.4_spmd.sunk | while | flops 268893696 | bytes 31679636 | solution.py:46
  473.2 16.0 %conditional.4 = ((f32[128,256,4]{1,0,2:T(8,128)}, f32[4,8192]{1,0:T(4,128)S(1)})) conditional(s32[]{:T(128)} %convert_element_type.90, (f32[128,256,4]{1,0,2:T(8,128)}, f32[4,8192]{1,0:T(4,128)S(1)}) %tuple.70, (s32[]{:T(128)}, s32[]{:T(128)}, bf16[4,8192]{1,0:T(4,128)(2,1)}, bf16[8,512,1024]{1,2,0:T(8,128)(2,1)}, s32[]{:T(128)}, ...), branch_computations={%region_1.1_spmd, %region_2.3_spmd} | conditional | flops 268893696 | bytes 31679430 | solution.py:79
  502.8 318.5 %reduce-scatter.4.cloned.1.call-done = bf16[128,4]{1,0:T(8,128)(2,1)} async-done(((bf16[4096,4]{1,0:T(8,128)(2,1)}), bf16[128,4]{1,0:T(8,128)(2,1)}) %reduce-scatter.4.cloned.1.call-update) | async-done | bytes 1040
  822.1 17.6 %psum.7 = f32[4,128]{1,0:T(4,128)S(1)} all-reduce(bf16[4,128]{1,0:T(4,128)(2,1)S(1)} %copy.50), channel_id=1, replica_groups=mesh['chan'=8,'ctx'=32] {'chan'}, use_global_device_ids=true, to_apply=%region_10.11 | all-reduce | flops 512 | bytes 3072 | tf_op jit(solution)/shard_map/psum | solution.py:106
  (171 shorter events, 172.2 us)
Async XLA Ops:
  7.2 4.5 copy-start.5
  7.2 5.3 copy-start.7
  7.2 109.0 %all-gather.5.cloned.1.call-start = ((), (), s32[]{:S(2)}) async-start(), calls=%async_computation.2 | async-start | bytes 8650752 | tf_op jit(solution)/shard_map/all_gather | solution.py:99
  8.4 115.2 %copy-start.1 = (bf16[128,1024]{0,1:T(8,128)(2,1)}, bf16[128,1024]{0,1:T(8,128)(2,1)S(1)}, u32[]{:S(2)}) copy-start(bf16[128,1024]{0,1:T(8,128)(2,1)S(1)} %copy.36) | copy-start | bytes 786436
  9.6 114.0 %copy-start.3 = (bf16[128,1024]{0,1:T(8,128)(2,1)}, bf16[128,1024]{0,1:T(8,128)(2,1)S(1)}, u32[]{:S(2)}) copy-start(bf16[128,1024]{0,1:T(8,128)(2,1)S(1)} %copy.39) | copy-start | bytes 786436
  10.4 453.2 %all-gather.3.cloned.1.call-start = ((), (), s32[]{:S(2)}) async-start(), calls=%async_computation.1 | async-start | bytes 8650752 | tf_op jit(solution)/shard_map/all_gather | solution.py:83
  362.6 108.5 %copy-start.6 = (bf16[4,8192]{1,0:T(4,128)(2,1)}, bf16[4,8192]{1,0:T(4,128)(2,1)S(1)}, u32[]{:S(2)}) copy-start(bf16[4,8192]{1,0:T(4,128)(2,1)S(1)} %get-tuple-element.458) | copy-start | bytes 196612
  362.6 2.3 copy-start
  364.7 456.6 %reduce-scatter.4.cloned.1.call-start = ((), (), s32[]{:S(2)}) async-start(), calls=%async_computation.3 | async-start | bytes 1081344
  498.1 2.8 copy-start.2
  498.1 2.8 copy-start.4
Sparse Core Ops, SparseCore 0:
  11.1 105.0 all-gather.4
  364.8 98.8 all-gather.2
  501.1 320.1 reduce-scatter.3
where the time goes:
time: 849 us; the launch traced here: 847 us
  waiting for transfers between devices  481 us (57%)
  local copies, waits for them, and re-layouts  259 us (31%)
  blocking collectives  56 us (7%)
  loops' own time  17.9 us (2%)
  matrix products  15.2 us (2%)
  between operations  14 us (2%)
    unnamed x4, waiting for transfers between devices  319 us
    all_gather x1, waiting for transfers between devices, shards(): lax.all_gather(gated, 'ctx', axis=0, tiled=True)  96.9 us
    cond x37, local copies, waits for them, and re-layouts  76.6 us
    all_gather x1, waiting for transfers between devices, shards(): lax.all_gather(back, 'ctx', axis=0, tiled=True)  65.4 us
    reshape x9, local copies, waits for them, and re-layouts, toeplitz(): return flat.reshape(padded.shape[0], height, span - 1)[:, :, :breadth]  56.2 us
    another operation x18, local copies, waits for them, and re-layouts, toeplitz(): tiled = jnp.tile(flipped, (1, height + 1))  43.2 us
    all_gather x1, blocking collectives, shards(): taps = lax.all_gather(filters, 'ctx', axis=1, tiled=True)  38.3 us
    slice x9, local copies, waits for them, and re-layouts, toeplitz(): flat = tiled[:, height - 1:height - 1 + height * (span - 1)]  24.4 us
  transfers between devices with their start and end apart: 3, of which 3 were waited for; matrix products, arithmetic and copies ran while one was open for 1% of the time, Pallas kernels for 0%

commit v1 on v0

--- a/solution.py
+++ b/solution.py
@@ -5,6 +5,12 @@
 
 D = 8192
 NFILT = 4
+
+
+def gather_from_all(x, axis, dim):
+    devices = lax.axis_size(axis)
+    repeats = [devices if d == dim else 1 for d in range(x.ndim)]
+    return lax.all_to_all(jnp.tile(x, repeats), axis, split_axis=dim, concat_axis=dim, tiled=True)
 
 
 def toeplitz(padded, base, height, breadth):
@@ -95,9 +101,7 @@
 
         return lax.cond(start + count > first, backward_work, lambda state: state, grad_acc)
 
-    grad_acc = in_blocks(
-        backward_block, empty, lax.all_gather(back, "ctx", axis=0, tiled=True), rows
-    )
+    grad_acc = in_blocks(backward_block, empty, gather_from_all(back, "ctx", 0), rows)
     mixed = mixed_acc.reshape(rows, width)
     gated_grad = grad_acc.reshape(rows, width)
     lag_share = lax.psum_scatter(

time: 849 us -> 989 us (1.16)
  blocking collectives: 56 us -> 237 us
  waiting for transfers between devices: 481 us -> 421 us
  starting transfers between devices: 0.3 us -> 12.6 us
    all_gather x1, blocking collectives: 38.3 us -> 219 us  [shards(): taps = lax.all_gather(filters, 'ctx', axis=1, tiled=True)]
    all_gather x1 -> x0, waiting for transfers between devices: 65.4 us -> none  [shards(): lax.all_gather(back, 'ctx', axis=0, tiled=True)]
    all_to_all x0 -> x1, starting transfers between devices: none -> 12.3 us  [gather_from_all(): lax.all_to_all(jnp.tile(x, repeats), axis, split_axis=dim, concat_axis=di...]
    while x3 -> x4, local copies, waits for them, and re-layouts: 1.72 us -> 13.2 us  [in_blocks(): result, unused = lax.scan(visit, carry, (parts, offsets))]
    unnamed x4 -> x3, waiting for transfers between devices: 319 us -> 319 us
  transfers between devices with their start and end apart: 3 -> 3, of which waited for: 3 -> 2; matrix products, arithmetic and copies ran while one was open for 1% -> 0% of each run, Pallas kernels for 0% -> 0%
where the time goes in v1:
time: 989 us; the launch traced here: 987 us
  waiting for transfers between devices  421 us (43%)
  local copies, waits for them, and re-layouts  267 us (27%)
  blocking collectives  237 us (24%)
  loops' own time  17 us (2%)
  matrix products  15.2 us (2%)
  between operations  14.3 us (1%)
  starting transfers between devices  12.6 us (1%)
    unnamed x3, waiting for transfers between devices  319 us
    all_gather x1, blocking collectives, shards(): taps = lax.all_gather(filters, 'ctx', axis=1, tiled=True)  219 us
    all_gather x1, waiting for transfers between devices, shards(): lax.all_gather(gated, 'ctx', axis=0, tiled=True)  102 us
    cond x37, local copies, waits for them, and re-layouts  76.7 us
    reshape x9, local copies, waits for them, and re-layouts, toeplitz(): return flat.reshape(padded.shape[0], height, span - 1)[:, :, :breadth]  56.3 us
    another operation x18, local copies, waits for them, and re-layouts, toeplitz(): tiled = jnp.tile(flipped, (1, height + 1))  43.2 us
    slice x9, local copies, waits for them, and re-layouts, toeplitz(): flat = tiled[:, height - 1:height - 1 + height * (span - 1)]  24.4 us
    dynamic_slice x25, local copies, waits for them, and re-layouts, in_blocks(): result, unused = lax.scan(visit, carry, (parts, offsets))  21.5 us
  transfers between devices with their start and end apart: 3, of which 2 were waited for; matrix products, arithmetic and copies ran while one was open for 0% of the time, Pallas kernels for 0%

profile of v1, /device:TPU:1, one launch (start us, length us, event | category | flops | bytes accessed | tf_op | source)
XLA Modules:
  0.0 987.0 jit_solution(17157121163048954796)
XLA Ops:
  14.1 12.3 %all-to-all-start = ((bf16[32,128,1024]{2,1,0:T(8,128)(2,1)}), bf16[32,128,1024]{2,1,0:T(8,128)(2,1)}, u32[]{:S(2)}, u32[]{:S(2)}) async-start(bf16[32,128,1024]{2,1,0:T(8,128)(2,1)} %tile.17), calls=%async_computation | async-start | bytes 16777216 | tf_op jit(solution)/shard_map/all_to_all | solution.py:13
  27.5 219.3 %all_gather.6 = bf16[4,4096]{1,0:T(4,128)(2,1)S(1)} all-gather(bf16[4,128]{1,0:T(4,128)(2,1)S(1)} %copy-done.9), channel_id=1, replica_groups=mesh['chan'=8,'ctx'=32] {'ctx'}, dimensions={1}, use_global_device_ids=true | all-gather | bytes 33792 | tf_op jit(solution)/shard_map/all_gather | solution.py:62
  246.8 11.5 %copy.63 = bf16[8,512,1024]{1,2,0:T(8,128)(2,1)} copy(bf16[8,512,1024]{2,1,0:T(8,128)(2,1)} %bitcast.7) | data formatting | bytes 16777216 | tf_op jit(solution)/shard_map/while | solution.py:52
  258.3 238.0 %while.27 = (s32[]{:T(128)}, f32[128,256,4]{1,0,2:T(8,128)S(1)}, s32[8]{0:T(128)S(1)}, s32[]{:T(128)}, bf16[4,8192]{1,0:T(4,128)(2,1)S(1)}, /*index=5*/bf16[8,512,1024]{1,2,0:T(8,128)(2,1)}, s32[]{:T(128)}, s32[]{:T(128)}) while((s32[]{:T(128)}, f32[128,256,4]{1,0,2:T(8,128)S(1)}, s32[8]{0:T(128)S(1)}, s32[]{:T(128)}, ...), condition=%wide.region_8.9_spmd, body=%wide.region_5.8_spmd.sunk | while | flops 134348800 | bytes 35643552 | solution.py:52
  259.7 28.4 %conditional.5 = (f32[128,256,4]{1,0,2:T(8,128)S(1)}) conditional(s32[]{:T(128)} %convert_element_type.91, f32[128,256,4]{1,0,2:T(8,128)S(1)} %get-tuple-element.413, (s32[]{:T(128)}, s32[]{:T(128)}, bf16[4,8192]{1,0:T(4,128)(2,1)S(1)}, bf16[8,512,1024]{1,2,0:T(8,128)(2,1)}, s32[]{:T(128)}, /*index=5*/f32[128,256,4]{1,0,2:T(8,128)S(1)}) %tuple.75), branch_computations={%region_6.6_spmd, %region_7.7_spmd} | conditional | flops 134348800 | bytes 35643384 | solution.py:102
  261.1 6.1 reshape.76
  278.1 6.9 reshape.62
  289.4 28.4 %conditional.5 = (f32[128,256,4]{1,0,2:T(8,128)S(1)}) conditional(s32[]{:T(128)} %convert_element_type.91, f32[128,256,4]{1,0,2:T(8,128)S(1)} %get-tuple-element.413, (s32[]{:T(128)}, s32[]{:T(128)}, bf16[4,8192]{1,0:T(4,128)(2,1)S(1)}, bf16[8,512,1024]{1,2,0:T(8,128)(2,1)}, s32[]{:T(128)}, /*index=5*/f32[128,256,4]{1,0,2:T(8,128)S(1)}) %tuple.75), branch_computations={%region_6.6_spmd, %region_7.7_spmd} | conditional | flops 134348800 | bytes 35643384 | solution.py:102
  290.9 6.1 reshape.76
  307.8 6.9 reshape.62
  319.2 28.4 %conditional.5 = (f32[128,256,4]{1,0,2:T(8,128)S(1)}) conditional(s32[]{:T(128)} %convert_element_type.91, f32[128,256,4]{1,0,2:T(8,128)S(1)} %get-tuple-element.413, (s32[]{:T(128)}, s32[]{:T(128)}, bf16[4,8192]{1,0:T(4,128)(2,1)S(1)}, bf16[8,512,1024]{1,2,0:T(8,128)(2,1)}, s32[]{:T(128)}, /*index=5*/f32[128,256,4]{1,0,2:T(8,128)S(1)}) %tuple.75), branch_computations={%region_6.6_spmd, %region_7.7_spmd} | conditional | flops 134348800 | bytes 35643384 | solution.py:102
  320.7 6.1 reshape.76
  337.6 6.9 reshape.62
  348.9 28.4 %conditional.5 = (f32[128,256,4]{1,0,2:T(8,128)S(1)}) conditional(s32[]{:T(128)} %convert_element_type.91, f32[128,256,4]{1,0,2:T(8,128)S(1)} %get-tuple-element.413, (s32[]{:T(128)}, s32[]{:T(128)}, bf16[4,8192]{1,0:T(4,128)(2,1)S(1)}, bf16[8,512,1024]{1,2,0:T(8,128)(2,1)}, s32[]{:T(128)}, /*index=5*/f32[128,256,4]{1,0,2:T(8,128)S(1)}) %tuple.75), branch_computations={%region_6.6_spmd, %region_7.7_spmd} | conditional | flops 134348800 | bytes 35643384 | solution.py:102
  350.4 6.1 reshape.76
  367.3 6.9 reshape.62
  378.7 28.4 %conditional.5 = (f32[128,256,4]{1,0,2:T(8,128)S(1)}) conditional(s32[]{:T(128)} %convert_element_type.91, f32[128,256,4]{1,0,2:T(8,128)S(1)} %get-tuple-element.413, (s32[]{:T(128)}, s32[]{:T(128)}, bf16[4,8192]{1,0:T(4,128)(2,1)S(1)}, bf16[8,512,1024]{1,2,0:T(8,128)(2,1)}, s32[]{:T(128)}, /*index=5*/f32[128,256,4]{1,0,2:T(8,128)S(1)}) %tuple.75), branch_computations={%region_6.6_spmd, %region_7.7_spmd} | conditional | flops 134348800 | bytes 35643384 | solution.py:102
  380.2 6.1 reshape.76
  397.1 6.9 reshape.62
  408.4 28.4 %conditional.5 = (f32[128,256,4]{1,0,2:T(8,128)S(1)}) conditional(s32[]{:T(128)} %convert_element_type.91, f32[128,256,4]{1,0,2:T(8,128)S(1)} %get-tuple-element.413, (s32[]{:T(128)}, s32[]{:T(128)}, bf16[4,8192]{1,0:T(4,128)(2,1)S(1)}, bf16[8,512,1024]{1,2,0:T(8,128)(2,1)}, s32[]{:T(128)}, /*index=5*/f32[128,256,4]{1,0,2:T(8,128)S(1)}) %tuple.75), branch_computations={%region_6.6_spmd, %region_7.7_spmd} | conditional | flops 134348800 | bytes 35643384 | solution.py:102
  409.9 6.1 reshape.76
  426.8 6.9 reshape.62
  438.2 28.4 %conditional.5 = (f32[128,256,4]{1,0,2:T(8,128)S(1)}) conditional(s32[]{:T(128)} %convert_element_type.91, f32[128,256,4]{1,0,2:T(8,128)S(1)} %get-tuple-element.413, (s32[]{:T(128)}, s32[]{:T(128)}, bf16[4,8192]{1,0:T(4,128)(2,1)S(1)}, bf16[8,512,1024]{1,2,0:T(8,128)(2,1)}, s32[]{:T(128)}, /*index=5*/f32[128,256,4]{1,0,2:T(8,128)S(1)}) %tuple.75), branch_computations={%region_6.6_spmd, %region_7.7_spmd} | conditional | flops 134348800 | bytes 35643384 | solution.py:102
  456.6 6.9 reshape.62
  467.9 28.4 %conditional.5 = (f32[128,256,4]{1,0,2:T(8,128)S(1)}) conditional(s32[]{:T(128)} %convert_element_type.91, f32[128,256,4]{1,0,2:T(8,128)S(1)} %get-tuple-element.413, (s32[]{:T(128)}, s32[]{:T(128)}, bf16[4,8192]{1,0:T(4,128)(2,1)S(1)}, bf16[8,512,1024]{1,2,0:T(8,128)(2,1)}, s32[]{:T(128)}, /*index=5*/f32[128,256,4]{1,0,2:T(8,128)S(1)}) %tuple.75), branch_computations={%region_6.6_spmd, %region_7.7_spmd} | conditional | flops 134348800 | bytes 35643384 | solution.py:102
  486.4 6.9 reshape.62
  500.6 102.5 %all-gather.2.cloned.1.call-done = bf16[4096,1024]{0,1:T(8,128)(2,1)} async-done(((bf16[128,1024]{0,1:T(8,128)(2,1)}), bf16[4096,1024]{0,1:T(8,128)(2,1)}) %all-gather.2.cloned.1.call-update) | async-done | bytes 8388624 | tf_op jit(solution)/shard_map/all_gather | solution.py:89
  603.1 7.4 copy.78
  611.4 26.2 %while.26 = (s32[]{:T(128)}, f32[128,256,4]{1,0,2:T(8,128)}, f32[4,8192]{1,0:T(4,128)S(1)}, s32[8]{0:T(128)S(1)}, s32[]{:T(128)}, /*index=5*/s32[]{:T(128)}, bf1...) while((s32[]{:T(128)}, f32[128,256,4]{1,0,2:T(8,128)}, ...), condition=%wide.region_4.5_spmd, body=%wide.region_0.4_spmd.sunk | while | flops 268893696 | bytes 31679636 | solution.py:52
  612.6 16.0 %conditional.4 = ((f32[128,256,4]{1,0,2:T(8,128)}, f32[4,8192]{1,0:T(4,128)S(1)})) conditional(s32[]{:T(128)} %convert_element_type.90, (f32[128,256,4]{1,0,2:T(8,128)}, f32[4,8192]{1,0:T(4,128)S(1)}) %tuple.72, (s32[]{:T(128)}, s32[]{:T(128)}, bf16[4,8192]{1,0:T(4,128)(2,1)}, bf16[8,512,1024]{1,2,0:T(8,128)(2,1)}, s32[]{:T(128)}, ...), branch_computations={%region_1.1_spmd, %region_2.3_spmd} | conditional | flops 268893696 | bytes 31679430 | solution.py:85
  642.2 318.9 %reduce-scatter.4.cloned.1.call-done = bf16[128,4]{1,0:T(8,128)(2,1)} async-done(((bf16[4096,4]{1,0:T(8,128)(2,1)}), bf16[128,4]{1,0:T(8,128)(2,1)}) %reduce-scatter.4.cloned.1.call-update) | async-done | bytes 1040
  961.9 17.6 %psum.7 = f32[4,128]{1,0:T(4,128)S(1)} all-reduce(bf16[4,128]{1,0:T(4,128)(2,1)S(1)} %copy.70), channel_id=1, replica_groups=mesh['chan'=8,'ctx'=32] {'chan'}, use_global_device_ids=true, to_apply=%region_10.11 | all-reduce | flops 512 | bytes 3072 | tf_op jit(solution)/shard_map/psum | solution.py:110
  (176 shorter events, 174.8 us)
Async XLA Ops:
  8.3 5.8 copy-start.2
  9.5 4.6 copy-start.4
  9.6 4.5 copy-start
  14.1 12.4 %copy-start.6 = (bf16[128,1024]{1,0:T(8,128)(2,1)S(1)}, bf16[128,1024]{1,0:T(8,128)(2,1)}, u32[]{:S(2)}) copy-start(bf16[128,1024]{1,0:T(8,128)(2,1)} %param.14) | copy-start | bytes 786436
  14.1 12.6 %copy-start.7 = (bf16[128,1024]{1,0:T(8,128)(2,1)S(1)}, bf16[128,1024]{1,0:T(8,128)(2,1)}, u32[]{:S(2)}) copy-start(bf16[128,1024]{1,0:T(8,128)(2,1)} %param.15) | copy-start | bytes 786436
  14.1 13.4 %copy-start.9 = (bf16[4,128]{1,0:T(4,128)(2,1)S(1)}, bf16[4,128]{1,0:T(4,128)(2,1)}, u32[]{:S(2)}) copy-start(bf16[4,128]{1,0:T(4,128)(2,1)} %param.16) | copy-start | bytes 3076
  14.1 232.7 %all-to-all-start = ((bf16[32,128,1024]{2,1,0:T(8,128)(2,1)}), bf16[32,128,1024]{2,1,0:T(8,128)(2,1)}, u32[]{:S(2)}, u32[]{:S(2)}) async-start(bf16[32,128,1024]{2,1,0:T(8,128)(2,1)} %tile.17), calls=%async_computation | async-start | bytes 16777216 | tf_op jit(solution)/shard_map/all_to_all | solution.py:13
  26.4 576.7 %all-gather.2.cloned.1.call-start = ((), (), s32[]{:S(2)}) async-start(), calls=%async_computation.2 | async-start | bytes 8650752 | tf_op jit(solution)/shard_map/all_gather | solution.py:89
  496.4 114.1 %copy-start.8 = (bf16[4,8192]{1,0:T(4,128)(2,1)}, bf16[4,8192]{1,0:T(4,128)(2,1)S(1)}, u32[]{:S(2)}) copy-start(bf16[4,8192]{1,0:T(4,128)(2,1)S(1)} %get-tuple-element.470) | copy-start | bytes 196612
  496.4 2.3 copy-start.1
  498.5 462.6 %reduce-scatter.4.cloned.1.call-start = ((), (), s32[]{:S(2)}) async-start(), calls=%async_computation.3 | async-start | bytes 1081344
  637.6 2.8 copy-start.3
  637.6 2.8 copy-start.5
Sparse Core Ops, SparseCore 0:
  498.6 104.4 all-gather.1
  640.5 320.5 reduce-scatter.3
